TPU v7x, 256 devices: a whole 4x4x8 slice. The times are simulated.
256 devices in a mesh: dap: 128 (over x_lo, y, z, core), dp: 2 (over x_hi).
Axes of the slice: x: 4 (x_hi: 2, x_lo: 2; x = x_hi * 2 + x_lo), y: 4, z: 8, core: 2. Of those that a mesh axis runs over, the one named last changes fastest.
Arguments:
- alignment_embedding: bfloat16 [256, 128, 256], P('dp', 'dap'), parts along dimension 0, may hold values from -6 to 6
- alignment_existing_flags: int32 [256, 128], P('dp', 'dap'), parts along dimension 0, may hold values 0 or 1
- couple_embedding: bfloat16 [256, 128, 128], P(('dp', 'dap')), parts along dimension 0, may hold values from -6 to 6
- alignment_scaling_factor: float32 [256], replicated, may hold values from 0.1 to 1.9
- couple_scaling_factor: float32 [128], replicated, may hold values from 0.1 to 1.9
- request_matrix: bfloat16 [256, 256], replicated, may hold values from -0.375 to 0.375
- lookup_matrix: bfloat16 [256, 256], replicated, may hold values from -0.375 to 0.375
- content_matrix: bfloat16 [256, 256], replicated, may hold values from -0.375 to 0.375
- switch_matrix: bfloat16 [256, 256], replicated, may hold values from -0.375 to 0.375
- final_projection_matrix: bfloat16 [256, 256], replicated, may hold values from -0.375 to 0.375
- couple_to_headterm_matrix: bfloat16 [128, 8], replicated, may hold values from -30 to 30
- increment_adjoint: bfloat16 [256, 128, 256], P('dp', 'dap'), parts along dimension 0, may hold values from -48 to 48
Outputs:
- alignment_increment: bfloat16 [256, 128, 256], P('dp', 'dap'), parts along dimension 0
- alignment_adjoint: bfloat16 [256, 128, 256], P('dp', 'dap'), parts along dimension 0
- couple_adjoint: bfloat16 [256, 128, 128], P(('dp', 'dap')), parts along dimension 0
- d_w_query: float32 [512, 256], P('dp'), parts along dimension 0
- d_w_key: float32 [512, 256], P('dp'), parts along dimension 0
- d_w_value: float32 [512, 256], P('dp'), parts along dimension 0
- d_w_gate: float32 [512, 256], P('dp'), parts along dimension 0
- d_w_out: float32 [512, 256], P('dp'), parts along dimension 0
- couple_headterm_adjoint: float32 [256, 8], P('dp'), parts along dimension 0
- d_msa_gain: float32 [512], P('dp'), parts along dimension 0
- couple_scaling_adjoint: float32 [256], P('dp'), parts along dimension 0
There are 2 independent parts, one for each index of `dp`. A program takes and returns all parts, laid end to end along the dimension named above; an argument that names none is the same for every part. Nothing has to cross between parts.
All inputs are finite; a program needn't handle non-finite values. No bound on the sum of `alignment_existing_flags` on one device may be relied on, other than what follows from the above.
Results may differ from a plain program's by a relative error of at most 0.012.
The roundings to bfloat16 on the way count: a program that leaves them out, or rounds other values in their place, can miss the bound.
Values may be sent and summed in bfloat16 or wider, within the bound.
No kernel may reach another device: no remote copies, remote signals or barrier semaphores. Data moves between devices by JAX's collectives and lax.ppermute only.
A program may use at most 64 MiB of HBM per device.

v0:
```python
import jax
import jax.numpy as jnp
from jax import lax
from jax.sharding import PartitionSpec as P

ALIGN_FEATURES = 256
HEAD_NUMBER = 8
HEAD_DIMENSION = 32
EPS = 1e-05


def standardise_features(value, gain):
    mean = jnp.mean(value, axis=-1, keepdims=True)
    centered = value - mean
    variance = jnp.mean(centered * centered, axis=-1, keepdims=True)
    reciprocal_spread = lax.rsqrt(variance + EPS)
    standardised_lines = centered * reciprocal_spread
    return (standardised_lines, reciprocal_spread, standardised_lines * gain)


def standardise_features_adjoint(upstream_gradient, standardised_lines, reciprocal_spread, gain):
    rescaled_request = upstream_gradient * gain
    return reciprocal_spread * (
        rescaled_request
        - jnp.mean(rescaled_request, axis=-1, keepdims=True)
        - standardised_lines
        * jnp.mean(rescaled_request * standardised_lines, axis=-1, keepdims=True)
    )


def tensor_product(left, right):
    return lax.dot_general(
        left, right, (((0,), (0,)), ((), ())), preferred_element_type=jnp.float32
    )


def onward_one_line(
    alignment_line_content,
    line_filter_flags,
    couple_headwise_terms,
    alignment_scaling_factor,
    request_matrix,
    lookup_matrix,
    content_matrix,
    switch_matrix,
    final_projection_matrix,
):
    element_number = alignment_line_content.shape[0]
    standardised_lines, reciprocal_spread, rescaled_request = standardise_features(
        alignment_line_content.astype(jnp.float32), alignment_scaling_factor
    )
    input_arrays = rescaled_request.astype(jnp.bfloat16)
    query = (
        jnp.dot(input_arrays, request_matrix, preferred_element_type=jnp.float32)
        * HEAD_DIMENSION ** (-0.5)
    ).astype(jnp.bfloat16)
    keys = jnp.dot(input_arrays, lookup_matrix, preferred_element_type=jnp.float32).astype(
        jnp.bfloat16
    )
    values = jnp.dot(input_arrays, content_matrix, preferred_element_type=jnp.float32).astype(
        jnp.bfloat16
    )
    gate_sigmoid = jax.nn.sigmoid(
        jnp.dot(input_arrays, switch_matrix, preferred_element_type=jnp.float32)
    )
    query = query.reshape(element_number, HEAD_NUMBER, HEAD_DIMENSION)
    keys = keys.reshape(element_number, HEAD_NUMBER, HEAD_DIMENSION)
    values = values.reshape(element_number, HEAD_NUMBER, HEAD_DIMENSION)
    scores = jnp.einsum("ihd,jhd->ihj", query, keys, preferred_element_type=jnp.float32)
    scores = (
        scores
        + couple_headwise_terms.astype(jnp.float32)
        + (1000000000.0 * (line_filter_flags.astype(jnp.float32) - 1.0))[None, None, :]
    )
    probs = jax.nn.softmax(scores, axis=-1)
    probs_low = probs.astype(jnp.bfloat16)
    attention_probs = jnp.einsum(
        "ihj,jhd->ihd", probs_low, values, preferred_element_type=jnp.float32
    ).reshape(element_number, HEAD_NUMBER * HEAD_DIMENSION)
    weighted_values = (gate_sigmoid * attention_probs).astype(jnp.bfloat16)
    alignment_increment = jnp.dot(
        weighted_values, final_projection_matrix, preferred_element_type=jnp.float32
    ).astype(jnp.bfloat16)
    kept_intermediates = (
        standardised_lines,
        reciprocal_spread,
        input_arrays,
        query,
        keys,
        values,
        gate_sigmoid,
        attention_probs,
        weighted_values,
        probs,
    )
    return (alignment_increment, kept_intermediates)


def reverse_one_line(
    line_adjoint_routine,
    kept_intermediates,
    alignment_scaling_factor,
    request_matrix,
    lookup_matrix,
    content_matrix,
    switch_matrix,
    final_projection_matrix,
):
    (
        standardised_lines,
        reciprocal_spread,
        input_arrays,
        query,
        keys,
        values,
        gate_sigmoid,
        attention_probs,
        weighted_values,
        probs,
    ) = kept_intermediates
    element_number = line_adjoint_routine.shape[0]
    probs_low = probs.astype(jnp.bfloat16)
    upstream_gradient = lax.dot_general(
        line_adjoint_routine,
        final_projection_matrix,
        (((1,), (1,)), ((), ())),
        preferred_element_type=jnp.float32,
    )
    d_attn = (upstream_gradient * gate_sigmoid).astype(jnp.bfloat16)
    gate_logit_gradient = (
        upstream_gradient * attention_probs * gate_sigmoid * (1.0 - gate_sigmoid)
    ).astype(jnp.bfloat16)
    d_attn_heads = d_attn.reshape(element_number, HEAD_NUMBER, HEAD_DIMENSION)
    d_probs = jnp.einsum("ihd,jhd->ihj", d_attn_heads, values, preferred_element_type=jnp.float32)
    affinity_adjoint = probs * (d_probs - jnp.sum(probs * d_probs, axis=-1, keepdims=True))
    d_low = affinity_adjoint.astype(jnp.bfloat16)
    query_gradient = (
        (
            jnp.einsum("ihj,jhd->ihd", d_low, keys, preferred_element_type=jnp.float32)
            * HEAD_DIMENSION ** (-0.5)
        )
        .astype(jnp.bfloat16)
        .reshape(element_number, HEAD_NUMBER * HEAD_DIMENSION)
    )
    key_gradient = (
        jnp.einsum("ihj,ihd->jhd", d_low, query, preferred_element_type=jnp.float32)
        .astype(jnp.bfloat16)
        .reshape(element_number, HEAD_NUMBER * HEAD_DIMENSION)
    )
    value_gradient = (
        jnp.einsum("ihj,ihd->jhd", probs_low, d_attn_heads, preferred_element_type=jnp.float32)
        .astype(jnp.bfloat16)
        .reshape(element_number, HEAD_NUMBER * HEAD_DIMENSION)
    )
    backward_result = (((1,), (1,)), ((), ()))
    argument_adjoints = lax.dot_general(
        query_gradient, request_matrix, backward_result, preferred_element_type=jnp.float32
    )
    argument_adjoints = argument_adjoints + lax.dot_general(
        key_gradient, lookup_matrix, backward_result, preferred_element_type=jnp.float32
    )
    argument_adjoints = argument_adjoints + lax.dot_general(
        value_gradient, content_matrix, backward_result, preferred_element_type=jnp.float32
    )
    argument_adjoints = argument_adjoints + lax.dot_general(
        gate_logit_gradient, switch_matrix, backward_result, preferred_element_type=jnp.float32
    )
    line_adjoint = standardise_features_adjoint(
        argument_adjoints, standardised_lines, reciprocal_spread, alignment_scaling_factor
    ).astype(jnp.bfloat16)
    matrix_adjoints = (
        tensor_product(input_arrays, query_gradient),
        tensor_product(input_arrays, key_gradient),
        tensor_product(input_arrays, value_gradient),
        tensor_product(input_arrays, gate_logit_gradient),
        tensor_product(weighted_values, line_adjoint_routine),
        jnp.sum(argument_adjoints * standardised_lines, axis=0),
    )
    return (line_adjoint, affinity_adjoint, matrix_adjoints)


def on_device(
    alignment_embedding,
    alignment_existing_flags,
    couple_embedding,
    alignment_scaling_factor,
    couple_scaling_factor,
    request_matrix,
    lookup_matrix,
    content_matrix,
    switch_matrix,
    final_projection_matrix,
    couple_to_headterm_matrix,
    increment_adjoint,
):
    filter_shared = alignment_existing_flags.astype(jnp.bfloat16)
    alignment_line_embedding, alignment_line_flags = (
        lax.all_to_all(alignment_embedding, "dap", split_axis=0, concat_axis=1, tiled=True),
        lax.all_to_all(filter_shared, "dap", split_axis=0, concat_axis=1, tiled=True),
    )
    pair_hat, pair_inv, pair_scaled = standardise_features(
        couple_embedding.astype(jnp.float32), couple_scaling_factor
    )
    pair_ln = pair_scaled.astype(jnp.bfloat16)
    bias_rows = jnp.einsum(
        "ijc,ch->ihj", pair_ln, couple_to_headterm_matrix, preferred_element_type=jnp.float32
    ).astype(jnp.bfloat16)
    couple_headwise_terms = lax.all_gather(bias_rows, "dap", axis=0, tiled=True)

    def onward_loop_step(carry, loop_elements):
        alignment_increment, kept_intermediates = onward_one_line(
            loop_elements[0],
            loop_elements[1],
            couple_headwise_terms,
            alignment_scaling_factor,
            request_matrix,
            lookup_matrix,
            content_matrix,
            switch_matrix,
            final_projection_matrix,
        )
        return (carry, (alignment_increment, kept_intermediates))

    unused_value, (row_updates, all_saved_residuals) = lax.scan(
        onward_loop_step, None, (alignment_line_embedding, alignment_line_flags)
    )
    update_out = lax.all_to_all(row_updates, "dap", split_axis=1, concat_axis=0, tiled=True)
    seq_grad = lax.all_to_all(increment_adjoint, "dap", split_axis=0, concat_axis=1, tiled=True)
    amino_positions = alignment_line_embedding.shape[1]
    span_length = HEAD_NUMBER * HEAD_DIMENSION
    blank_matrix = (
        jnp.zeros((ALIGN_FEATURES, span_length), jnp.float32),
        jnp.zeros((ALIGN_FEATURES, span_length), jnp.float32),
        jnp.zeros((ALIGN_FEATURES, span_length), jnp.float32),
        jnp.zeros((ALIGN_FEATURES, span_length), jnp.float32),
        jnp.zeros((span_length, ALIGN_FEATURES), jnp.float32),
        jnp.zeros((ALIGN_FEATURES,), jnp.float32),
    )

    def backward_step(carry, loop_elements):
        bias_sum, subtotal_list = carry
        line_adjoint, affinity_adjoint, matrix_adjoints = reverse_one_line(
            loop_elements[0],
            loop_elements[1],
            alignment_scaling_factor,
            request_matrix,
            lookup_matrix,
            content_matrix,
            switch_matrix,
            final_projection_matrix,
        )
        subtotal_list = tuple((a + b for a, b in zip(subtotal_list, matrix_adjoints)))
        return ((bias_sum + affinity_adjoint, subtotal_list), line_adjoint)

    beginning_shift = (
        jnp.zeros((amino_positions, HEAD_NUMBER, amino_positions), jnp.float32),
        blank_matrix,
    )
    (bias_term, subtotal_list), line_adjoint_list = lax.scan(
        backward_step, beginning_shift, (seq_grad, all_saved_residuals)
    )
    additive_term_adjoint = lax.psum_scatter(bias_term, "dap", scatter_dimension=0, tiled=True)
    d_pln = jnp.einsum(
        "ihj,ch->ijc",
        additive_term_adjoint,
        couple_to_headterm_matrix.astype(jnp.float32),
        precision=lax.Precision.HIGHEST,
    )
    w_bias_part = jnp.einsum(
        "ijc,ihj->ch",
        pair_ln.astype(jnp.float32),
        additive_term_adjoint,
        precision=lax.Precision.HIGHEST,
    )
    pair_gain_part = jnp.sum(d_pln * pair_hat, axis=(0, 1))
    couple_adjoint = standardise_features_adjoint(
        d_pln, pair_hat, pair_inv, couple_scaling_factor
    ).astype(jnp.bfloat16)
    totals = lax.psum(
        (
            subtotal_list[0],
            subtotal_list[1],
            subtotal_list[2],
            subtotal_list[3],
            subtotal_list[4],
            w_bias_part,
            subtotal_list[5],
            pair_gain_part,
        ),
        "dap",
    )
    alignment_adjoint = lax.all_to_all(
        line_adjoint_list, "dap", split_axis=1, concat_axis=0, tiled=True
    )
    return (
        update_out,
        alignment_adjoint,
        couple_adjoint,
        totals[0],
        totals[1],
        totals[2],
        totals[3],
        totals[4],
        totals[5],
        totals[6],
        totals[7],
    )


def solution(mesh):
    in_specs = (
        P("dp", "dap", None),
        P("dp", "dap"),
        P(("dp", "dap"), None, None),
        P(),
        P(),
        P(),
        P(),
        P(),
        P(),
        P(),
        P(),
        P("dp", "dap", None),
    )
    out_specs = (
        P("dp", "dap", None),
        P("dp", "dap", None),
        P(("dp", "dap"), None, None),
        P("dp", None),
        P("dp", None),
        P("dp", None),
        P("dp", None),
        P("dp", None),
        P("dp", None),
        P("dp"),
        P("dp"),
    )
    return jax.shard_map(
        on_device, mesh=mesh, in_specs=in_specs, out_specs=out_specs, check_vma=False
    )
```

profile of v0, /device:TPU:4, one launch (start us, length us, event | category | flops | bytes accessed | tf_op | source)
XLA Modules:
  0.0 1600.0 jit_solution(11764958021694046716)
XLA Ops:
  7.2 0.7 convert_bitcast_fusion.2
  7.9 0.8 copy.78
  8.7 14.1 all-to-all-start.1
  23.0 0.6 copy-done.15
  23.8 157.6 %all-gather = bf16[1024,128]{1,0:T(8,128)(2,1)S(1)} all-gather(bf16[8,128]{1,0:T(8,128)(2,1)S(1)} %fusion.11), channel_id=2, replica_groups=mesh['dap'=128,'dp'=2] {'dap'}, dimensions={0}, use_global_device_ids=true | all-gather | bytes 264192 | tf_op jit(solution)/shard_map/all_gather | solution.py:208
  181.4 0.5 broadcast.220
  182.0 0.7 reduce.9
  182.6 0.7 reshape.335
  183.3 6.1 all-to-all-start
  189.5 0.8 copy-done.11
  190.3 0.7 reduce.8
  190.9 0.7 reshape.339
  191.8 1.0 multiply_reduce_fusion.2
  192.9 6.9 all-to-all-done
  199.7 6.1 all-to-all-start.3
  206.3 0.6 copy-done.8
  207.3 0.8 copy-done.7
  208.5 0.8 copy-done.9
  209.9 0.5 fusion.75
  210.7 5.5 all-to-all-done.3
  217.9 1.0 copy.89
  218.9 1.0 fusion.67
  219.9 1.0 fusion.65
  220.9 1.0 fusion.63
  221.9 1.0 fusion.69
  222.9 0.9 fusion.50
  224.2 1.0 reduce.10
  225.2 0.7 reshape.337
  225.8 8.0 all-to-all-start.2
  235.0 1.0 reduce.11
  236.1 0.6 reshape.341
  236.7 7.6 all-to-all-done.2
  244.3 6.1 all-to-all-start.4
  250.4 0.7 copy-done.16
  251.0 0.6 dynamic-slice.6
  251.7 0.6 copy.112
  252.3 8.6 all-to-all-done.4
  260.9 0.6 copy.111
  261.5 1041.0 %all-reduce.5.cloned.1.call-done = (f32[128,8,128]{2,1,0:T(8,128)}, f32[256,256]{1,0:T(8,128)}, f32[256,256]{1,0:T(8,128)}, f32[256,256]{1,0:T(8,128)}, f32[256,256]{1,0:T(8,128)}, /*index=5*/f32[256,256]{1,0:T(8,128)}) async-done(((f32[128,8,128]{2,1,0:T(8,128)}, f32[256,256]{1,0:T(8,128)}, f32[256,256]{1,0:T(8,128)}, f32[256,256]{1,0:T(8,128)}, f32[256,256]{1,0:T(8,128)}, ...) | async-done | bytes 1835024
  1302.6 1.7 fusion.46
  1304.3 1.5 fusion.57
  1306.1 0.7 copy.90
  1306.8 281.5 %all-reduce.1 = (f32[128,8]{0,1:T(8,128)}, f32[256]{0:T(256)}, f32[128]{0:T(128)}) all-reduce(f32[128,8]{0,1:T(8,128)S(1)} %fusion.57, f32[256]{0:T(256)S(1)} %get-tuple-element.196, f32[128]{0:T(128)S(1)} %get-tuple-element.199), channel_id=1, replica_groups=mesh['dap'=128,'dp'=2] {'dap'}, use_global_device_ids=true, to_apply=%region_17.18 | all-reduce | flops 1408 | bytes 11264 | tf_op jit(solution)/shard_map/psum | solution.py:279
  1588.3 0.7 copy.123
  1589.3 0.7 copy.124
  1590.4 0.7 copy.125
  1591.4 0.7 copy.126
  1592.4 0.7 copy.127
  (76 shorter events, 7.6 us)
Async XLA Ops:
  7.2 209.3 %copy-start = (bf16[256,256]{1,0:T(8,128)(2,1)S(1)}, bf16[256,256]{1,0:T(8,128)(2,1)}, u32[]{:S(2)}) copy-start(bf16[256,256]{1,0:T(8,128)(2,1)} %param.20) | copy-start | bytes 393220
  8.7 14.1 copy-start.13
  8.7 174.6 %all-to-all-start.1 = ((bf16[128,1,1]{2,1,0:T(2,128)(2,1)}), bf16[128,1,1]{2,1,0:T(2,128)(2,1)S(1)}, u32[]{:S(2)}, u32[]{:S(2)}) async-start(bf16[128,1,1]{2,1,0:T(2,128)(2,1)} %copy.78), calls=%async_computation.1 | async-start | bytes 131072 | tf_op jit(solution)/shard_map/all_to_all | solution.py:199
  22.9 0.7 copy-start.15
  23.0 0.7 copy-start.14
  23.8 158.1 %copy-start.10 = (bf16[128,1,256]{2,0,1:T(8,128)(2,1)S(1)}, bf16[128,1,256]{2,0,1:T(8,128)(2,1)}, u32[]{:S(2)}) copy-start(bf16[128,1,256]{2,0,1:T(8,128)(2,1)} %param.12) | copy-start | bytes 196612
  183.3 16.5 %all-to-all-start = ((bf16[128,2,128]{2,1,0:T(2,128)(2,1)}), bf16[128,2,128]{2,1,0:T(2,128)(2,1)S(1)}, u32[]{:S(2)}, u32[]{:S(2)}) async-start(bf16[128,2,128]{2,1,0:T(2,128)(2,1)} %reshape.335), calls=%async_computation | async-start | bytes 131072 | tf_op jit(solution)/shard_map/all_to_all | solution.py:198
  189.4 0.8 copy-start.11
  199.7 16.5 %all-to-all-start.3 = ((bf16[128,2,128]{2,1,0:T(2,128)(2,1)}), bf16[128,2,128]{2,1,0:T(2,128)(2,1)S(1)}, u32[]{:S(2)}, u32[]{:S(2)}) async-start(bf16[128,2,128]{2,1,0:T(2,128)(2,1)} %reshape.339), calls=%async_computation.3 | async-start | bytes 131072 | tf_op jit(solution)/shard_map/all_to_all | solution.py:228
  205.9 1096.7 %all-reduce.5.cloned.1.call-start = ((), (), s32[]{:S(2)}) async-start(), calls=%async_computation.5 | async-start | bytes 3670016
  206.0 0.9 copy-start.8
  206.3 0.7 copy-start.12
  207.2 0.9 copy-start.7
  208.3 0.9 copy-start.9
  210.7 5.5 copy-start.1
  225.8 18.4 %all-to-all-start.2 = ((bf16[128,2,128]{2,1,0:T(2,128)(2,1)}), bf16[128,2,128]{2,1,0:T(2,128)(2,1)S(1)}, u32[]{:S(2)}, u32[]{:S(2)}) async-start(bf16[128,2,128]{2,1,0:T(2,128)(2,1)} %reshape.337), calls=%async_computation.2 | async-start | bytes 131072 | tf_op jit(solution)/shard_map/all_to_all | solution.py:227
  244.3 16.6 %all-to-all-start.4 = ((bf16[128,2,128]{2,1,0:T(2,128)(2,1)}), bf16[128,2,128]{2,1,0:T(2,128)(2,1)S(1)}, u32[]{:S(2)}, u32[]{:S(2)}) async-start(bf16[128,2,128]{2,1,0:T(2,128)(2,1)} %reshape.341), calls=%async_computation.4 | async-start | bytes 131072 | tf_op jit(solution)/shard_map/all_to_all | solution.py:292
  250.4 0.7 copy-start.16
  1302.6 285.7 %copy-start.6 = (f32[256,256]{1,0:T(8,128)S(1)}, f32[256,256]{1,0:T(8,128)}, u32[]{:S(2)}) copy-start(f32[256,256]{1,0:T(8,128)} %get-tuple-element.228) | copy-start | bytes 786436
  1588.3 1.0 copy-start.5
  1589.3 1.0 copy-start.4
  1590.4 1.0 copy-start.3
  1591.4 1.0 copy-start.2
Sparse Core Ops, SparseCore 0:
  224.0 1078.5 all-reduce.4
where the time goes:
time: 1600 us
  waiting for transfers between devices  1070 us (67%)
  blocking collectives  439 us (27%)
  starting transfers between devices  40.5 us (3%)
  local copies, waits for them, and re-layouts  18 us (1%)
    unnamed x2, waiting for transfers between devices  1040 us
    psum x1, blocking collectives, on_device(): lax.psum((subtotal_list[0], subtotal_list[1], subtotal_list[2], subtotal_...  281 us
    all_gather x1, blocking collectives, on_device(): couple_headwise_terms = lax.all_gather(bias_rows, 'dap', axis=0, tiled=True)  158 us
  transfers between devices with their start and end apart: 6, of which 5 were waited for; matrix products, arithmetic and copies ran while one was open for 1% of the time, Pallas kernels for 0%

commit v1 on v0

--- a/solution.py
+++ b/solution.py
@@ -205,7 +205,10 @@
     bias_rows = jnp.einsum(
         "ijc,ch->ihj", pair_ln, couple_to_headterm_matrix, preferred_element_type=jnp.float32
     ).astype(jnp.bfloat16)
-    couple_headwise_terms = lax.all_gather(bias_rows, "dap", axis=0, tiled=True)
+    size = lax.axis_size("dap")
+    blocks = jnp.stack([bias_rows for _ in range(size)])
+    blocks = lax.all_to_all(blocks, "dap", split_axis=0, concat_axis=0)
+    couple_headwise_terms = jnp.concatenate(blocks, axis=0)
 
     def onward_loop_step(carry, loop_elements):
         alignment_increment, kept_intermediates = onward_one_line(

time: 1600 us -> 1470 us (0.919)
  blocking collectives: 439 us -> 281 us
  waiting for transfers between devices: 1070 us -> 1090 us
    all_gather x1 -> x0, blocking collectives: 158 us -> none  [on_device(): couple_headwise_terms = lax.all_gather(bias_rows, 'dap', axis=0, tiled=True)]
  transfers between devices with their start and end apart: 6 -> 7, of which waited for: 5 -> 7; matrix products, arithmetic and copies ran while one was open for 1% -> 1% of each run, Pallas kernels for 0% -> 0%
where the time goes in v1:
time: 1470 us
  waiting for transfers between devices  1090 us (74%)
  blocking collectives  281 us (19%)
  starting transfers between devices  45.7 us (3%)
  local copies, waits for them, and re-layouts  18 us (1%)
    unnamed x2, waiting for transfers between devices  1040 us
    psum x1, blocking collectives, on_device(): lax.psum((subtotal_list[0], subtotal_list[1], subtotal_list[2], subtotal_...  281 us
  transfers between devices with their start and end apart: 7, of which 7 were waited for; matrix products, arithmetic and copies ran while one was open for 1% of the time, Pallas kernels for 0%

profile of v1, /device:TPU:4, one launch (start us, length us, event | category | flops | bytes accessed | tf_op | source)
XLA Modules:
  0.0 1470.8 jit_solution(9994232051850191990)
XLA Ops:
  7.2 0.7 convert_bitcast_fusion.2
  7.9 0.8 copy.77
  8.7 14.1 all-to-all-start.2
  23.6 0.7 reduce.9
  24.3 0.7 reshape.340
  24.9 8.1 all-to-all-done.2
  33.1 6.1 all-to-all-start
  39.4 0.6 copy-done.11
  40.1 0.7 reduce.8
  40.7 0.7 reshape.344
  41.4 1.0 multiply_reduce_fusion.2
  42.4 7.1 all-to-all-done
  49.5 6.1 all-to-all-start.4
  56.1 0.6 copy-done.8
  56.9 9.0 all-to-all-done.4
  66.0 0.7 stack.2
  66.7 6.3 all-to-all-start.1
  73.7 0.7 copy-done.9
  74.8 0.9 copy-done.1
  75.9 10.1 all-to-all-done.1
  88.9 1.0 copy.88
  89.9 1.0 fusion.67
  90.9 1.0 fusion.65
  91.9 1.0 fusion.63
  92.9 1.0 fusion.69
  93.9 0.9 fusion.50
  95.1 1.0 reduce.10
  96.2 0.7 reshape.342
  96.8 6.7 all-to-all-start.3
  104.7 1.0 reduce.11
  105.8 0.6 reshape.346
  106.4 7.5 all-to-all-done.3
  113.9 6.1 all-to-all-start.5
  120.0 0.7 copy-done.16
  120.6 0.6 dynamic-slice.6
  121.3 0.6 copy.111
  121.9 8.4 all-to-all-done.5
  130.3 0.6 copy.110
  131.0 1042.4 %all-reduce.5.cloned.1.call-done = (f32[128,8,128]{2,1,0:T(8,128)}, f32[256,256]{1,0:T(8,128)}, f32[256,256]{1,0:T(8,128)}, f32[256,256]{1,0:T(8,128)}, f32[256,256]{1,0:T(8,128)}, /*index=5*/f32[256,256]{1,0:T(8,128)}) async-done(((f32[128,8,128]{2,1,0:T(8,128)}, f32[256,256]{1,0:T(8,128)}, f32[256,256]{1,0:T(8,128)}, f32[256,256]{1,0:T(8,128)}, f32[256,256]{1,0:T(8,128)}, ...) | async-done | bytes 1835024
  1173.4 1.7 fusion.46
  1175.1 1.5 fusion.57
  1176.9 0.7 copy.89
  1177.6 281.5 %all-reduce.1 = (f32[128,8]{0,1:T(8,128)}, f32[256]{0:T(256)}, f32[128]{0:T(128)}) all-reduce(f32[128,8]{0,1:T(8,128)S(1)} %fusion.57, f32[256]{0:T(256)S(1)} %get-tuple-element.196, f32[128]{0:T(128)S(1)} %get-tuple-element.199), channel_id=1, replica_groups=mesh['dap'=128,'dp'=2] {'dap'}, use_global_device_ids=true, to_apply=%region_17.18 | all-reduce | flops 1408 | bytes 11264 | tf_op jit(solution)/shard_map/psum | solution.py:282
  1459.1 0.7 copy.122
  1460.1 0.7 copy.123
  1461.2 0.7 copy.124
  1462.2 0.7 copy.125
  1463.3 0.7 copy.126
  (76 shorter events, 8.9 us)
Async XLA Ops:
  7.2 80.0 %copy-start = (bf16[256,256]{1,0:T(8,128)(2,1)S(1)}, bf16[256,256]{1,0:T(8,128)(2,1)}, u32[]{:S(2)}) copy-start(bf16[256,256]{1,0:T(8,128)(2,1)} %param.20) | copy-start | bytes 393220
  8.7 14.1 copy-start.13
  8.7 24.4 %all-to-all-start.2 = ((bf16[128,1,1]{2,1,0:T(2,128)(2,1)}), bf16[128,1,1]{2,1,0:T(2,128)(2,1)S(1)}, u32[]{:S(2)}, u32[]{:S(2)}) async-start(bf16[128,1,1]{2,1,0:T(2,128)(2,1)} %copy.77), calls=%async_computation.2 | async-start | bytes 131072 | tf_op jit(solution)/shard_map/all_to_all | solution.py:199
  22.8 0.8 copy-start.10
  24.9 14.3 copy-start.14
  24.9 14.3 copy-start.15
  33.1 16.5 %all-to-all-start = ((bf16[128,2,128]{2,1,0:T(2,128)(2,1)}), bf16[128,2,128]{2,1,0:T(2,128)(2,1)S(1)}, u32[]{:S(2)}, u32[]{:S(2)}) async-start(bf16[128,2,128]{2,1,0:T(2,128)(2,1)} %reshape.340), calls=%async_computation | async-start | bytes 131072 | tf_op jit(solution)/shard_map/all_to_all | solution.py:198
  39.2 0.8 copy-start.11
  49.5 16.5 %all-to-all-start.4 = ((bf16[128,2,128]{2,1,0:T(2,128)(2,1)}), bf16[128,2,128]{2,1,0:T(2,128)(2,1)S(1)}, u32[]{:S(2)}, u32[]{:S(2)}) async-start(bf16[128,2,128]{2,1,0:T(2,128)(2,1)} %reshape.344), calls=%async_computation.4 | async-start | bytes 131072 | tf_op jit(solution)/shard_map/all_to_all | solution.py:231
  55.7 0.9 copy-start.8
  56.0 0.7 copy-start.12
  66.7 6.5 copy-start.7
  66.7 19.2 %all-to-all-start.1 = ((bf16[128,1,8,128]{3,2,1,0:T(8,128)(2,1)}), bf16[128,1,8,128]{3,2,1,0:T(8,128)(2,1)S(1)}, u32[]{:S(2)}, u32[]{:S(2)}) async-start(bf16[128,1,8,128]{3,2,1,0:T(8,128)(2,1)} %stack.2), calls=%async_computation.1 | async-start | bytes 524288 | tf_op jit(solution)/shard_map/all_to_all | solution.py:210
  73.0 1100.4 %all-reduce.5.cloned.1.call-start = ((), (), s32[]{:S(2)}) async-start(), calls=%async_computation.6 | async-start | bytes 3670016
  73.5 0.9 copy-start.9
  74.8 0.9 copy-start.1
  96.8 17.1 %all-to-all-start.3 = ((bf16[128,2,128]{2,1,0:T(2,128)(2,1)}), bf16[128,2,128]{2,1,0:T(2,128)(2,1)S(1)}, u32[]{:S(2)}, u32[]{:S(2)}) async-start(bf16[128,2,128]{2,1,0:T(2,128)(2,1)} %reshape.342), calls=%async_computation.3 | async-start | bytes 131072 | tf_op jit(solution)/shard_map/all_to_all | solution.py:230
  113.9 16.4 %all-to-all-start.5 = ((bf16[128,2,128]{2,1,0:T(2,128)(2,1)}), bf16[128,2,128]{2,1,0:T(2,128)(2,1)S(1)}, u32[]{:S(2)}, u32[]{:S(2)}) async-start(bf16[128,2,128]{2,1,0:T(2,128)(2,1)} %reshape.346), calls=%async_computation.5 | async-start | bytes 131072 | tf_op jit(solution)/shard_map/all_to_all | solution.py:295
  120.0 0.7 copy-start.16
  1173.4 285.7 %copy-start.6 = (f32[256,256]{1,0:T(8,128)S(1)}, f32[256,256]{1,0:T(8,128)}, u32[]{:S(2)}) copy-start(f32[256,256]{1,0:T(8,128)} %get-tuple-element.228) | copy-start | bytes 786436
  1459.1 1.0 copy-start.5
  1460.1 1.0 copy-start.4
  1461.2 1.0 copy-start.3
  1462.2 1.0 copy-start.2
Sparse Core Ops, SparseCore 0:
  95.0 1078.3 all-reduce.4
